TPU v7x, 256 devices: a whole 4x4x8 slice. The times are simulated.
256 devices in a mesh: tm: 32 (over x, y, core), neur: 8 (over z).
Axes of the slice: x: 4, y: 4, z: 8, core: 2. Of those that a mesh axis runs over, the one named last changes fastest.
Arguments:
- activity: bfloat16 [51200, 12288], P('neur', 'tm'), may hold values from 0.01 to 1001, as said below
- patterns: bfloat16 [51200, 512], P('neur'), may hold values from 6.25e-05 to 0.08125, as said below
- loadings: bfloat16 [32, 12288], P(None, 'tm'), may hold values from 0.01 to 4.4, as said below
Outputs:
- h_next: float32 [32, 12288], P(None, 'tm')
- w_next: float32 [51200, 512], P(('neur', 'tm'))
- misfit: float32 [12288], P('tm')
Inputs may be any that keep to these rules, and one draw needn't show every extreme that they name: `activity`: positive. `patterns`: positive. `loadings`: positive.
All inputs are finite; a program needn't handle non-finite values.
Results may differ from a plain program's by a relative error of at most 0.0009.
Values may be sent and summed in bfloat16 or wider, within the bound.
A program may use at most 128 MiB of HBM per device.

v0:
```python
import jax
import jax.numpy as jnp
from jax import lax
from jax.sharding import PartitionSpec as P

RANK = 32
LAGS = 16


def passed_along(value, axis, steps):
    count = lax.axis_size(axis)
    leading, last = (max(0, -steps), min(count, count - steps))
    return lax.ppermute(value, axis, [(source, source + steps) for source in range(leading, last)])


def lag_stack(factor, rim):
    extended = jnp.concatenate([rim, factor], axis=1)
    width = factor.shape[1]
    rows = [extended[:, LAGS - 1 - lag : LAGS - 1 - lag + width] for lag in range(LAGS)]
    return jnp.concatenate(rows, axis=0)


def body(activity, patterns, loadings):
    span = loadings.shape[1]
    local_rows = patterns.shape[0]
    rim = passed_along(loadings[:, span - (LAGS - 1) :], "tm", 1)
    stacked = lag_stack(loadings, rim)
    recon = jnp.dot(patterns, stacked, preferred_element_type=jnp.float32)
    ratio = (activity.astype(jnp.float32) / recon).astype(jnp.bfloat16)
    ratio_next = passed_along(ratio[:, : LAGS - 1], "tm", -1)
    extended = jnp.concatenate([ratio, ratio_next], axis=1)
    gram = lax.dot_general(
        patterns, extended, (((0,), (0,)), ((), ())), preferred_element_type=jnp.float32
    )
    layered = gram.reshape(LAGS, RANK, span + LAGS - 1)
    numer = layered[0, :, 0:span]
    for lag in range(1, LAGS):
        numer = numer + layered[lag, :, lag : lag + span]
    colsum = jnp.sum(jnp.sum(patterns, axis=0, dtype=jnp.float32).reshape(LAGS, RANK), axis=0)
    numer_all, colsum_all = lax.psum((numer, colsum), "neur")
    h_next = loadings.astype(jnp.float32) * numer_all / colsum_all[:, None]
    fresh = h_next.astype(jnp.bfloat16)
    fresh_prev = passed_along(fresh[:, span - (LAGS - 1) :], "tm", 1)
    stacked_new = lag_stack(fresh, fresh_prev)
    act_wide = activity.astype(jnp.float32)
    recon_new = jnp.dot(patterns, stacked_new, preferred_element_type=jnp.float32)
    diverge = jnp.sum(act_wide * jnp.log(act_wide / recon_new) - act_wide + recon_new, axis=0)
    mass = jnp.sum(act_wide, axis=0)
    ratio_new = (act_wide / recon_new).astype(jnp.bfloat16)
    diverge_all, mass_all = lax.psum((diverge, mass), "neur")
    misfit = diverge_all / mass_all
    own_count = local_rows // lax.axis_size("tm")
    lag_part = jnp.sum(stacked_new, axis=1, dtype=jnp.float32)
    lagsum = lax.psum(lag_part, "tm")
    pnum = lax.psum_scatter(
        lax.dot_general(
            ratio_new, stacked_new, (((1,), (1,)), ((), ())), preferred_element_type=jnp.float32
        ),
        "tm",
        scatter_dimension=0,
        tiled=True,
    )
    own_patterns = lax.dynamic_slice_in_dim(
        patterns, lax.axis_index("tm") * own_count, own_count, 0
    )
    w_next = own_patterns.astype(jnp.float32) * pnum / lagsum[None, :]
    return (h_next, w_next, misfit)


def solution(mesh):
    return jax.shard_map(
        body,
        mesh=mesh,
        in_specs=(P("neur", "tm"), P("neur", None), P(None, "tm")),
        out_specs=(P(None, "tm"), P(("neur", "tm"), None), P("tm")),
        check_vma=False,
    )
```

profile of v0, /device:TPU:1, one launch (start us, length us, event | category | flops | bytes accessed | tf_op | source)
XLA Modules:
  0.0 218.1 jit_solution(12868446539411816418)
XLA Ops:
  7.2 0.8 slice.147
  8.0 4.6 %collective-permute-start = (bf16[32,15]{1,0:T(8,128)(2,1)S(1)}, bf16[32,15]{1,0:T(8,128)(2,1)S(1)}, u32[]{:S(2)}, u32[]{:S(2)}) collective-permute-start(bf16[32,15]{1,0:T(8,128)(2,1)S(1)} %slice.147), channel_id=1, source_target_pairs={{0,8},{8,16},{16,24},{24,32},{32,40},{40,48},{48,56},{56,64},{64,7... | collective-permute-start | bytes 2888 | tf_op jit(solution)/shard_map/ppermute | solution.py:13
  12.6 0.7 constant_dynamic-update-slice_fusion.15
  13.3 7.5 %copy.25 = bf16[6400,384]{0,1:T(8,128)(2,1)} copy(bf16[6400,384]{1,0:T(8,128)(2,1)} %param.3) | data formatting | bytes 9830400 | tf_op args[0]
  21.0 0.1 constant_dynamic-update-slice_fusion.12
  21.1 0.1 constant_dynamic-update-slice_fusion.11
  21.2 0.1 constant_dynamic-update-slice_fusion.10
  21.5 0.1 constant_dynamic-update-slice_fusion.7
  21.5 0.1 constant_dynamic-update-slice_fusion.6
  21.6 0.1 constant_dynamic-update-slice_fusion.5
  21.7 0.1 constant_dynamic-update-slice_fusion.4
  21.8 0.1 constant_dynamic-update-slice_fusion.3
  21.9 0.1 constant_dynamic-update-slice_fusion.2
  22.0 0.1 constant_dynamic-update-slice_fusion.1
  22.1 0.1 constant_dynamic-update-slice_fusion
  22.2 7.8 %fusion = bf16[6400,384]{0,1:T(8,128)(2,1)S(1)} fusion(bf16[6400,384]{0,1:T(8,128)(2,1)} %copy.25, bf16[512,384]{1,0:T(8,128)(2,1)S(1)} %constant_dynamic-update-slice_fusion, bf16[6400,512]{1,0:T(8,128)(2,1)} %param.4), kind=kOutput, calls=%fused_computation.8 | convolution fusion | flops 2523955200 | bytes 16777216 | tf_op jit(solution)/shard_map/dot_general | solution.py:28
  30.0 1.9 collective-permute-start.1
  31.9 0.3 copy-done.1
  32.2 0.9 convert_reduce_fusion.1
  33.2 3.8 %collective-permute-done.1 = bf16[6400,15]{0,1:T(8,128)(2,1)S(1)} collective-permute-done((bf16[6400,15]{0,1:T(8,128)(2,1)S(1)}, bf16[6400,15]{0,1:T(8,128)(2,1)S(1)}, u32[]{:S(2)}, u32[]{:S(2)}) %collective-permute-start.1) | collective-permute-done | bytes 192032 | tf_op jit(solution)/shard_map/ppermute | solution.py:13
  37.1 6.8 %fusion.9 = f32[512,399]{0,1:T(8,128)S(1)} fusion(bf16[6400,512]{1,0:T(8,128)(2,1)} %param.4, bf16[6400,15]{0,1:T(8,128)(2,1)S(1)} %collective-permute-done.1, bf16[6400,384]{0,1:T(8,128)(2,1)} %copy-done.1), kind=kOutput, calls=%fused_computation.17 | convolution fusion | flops 2625100800 | bytes 12477952 | tf_op jit(solution)/shard_map/dot_general | solution.py:32
  43.9 0.3 copy.26
  44.2 0.3 fusion.12
  44.5 26.0 %all-reduce.1 = (f32[32,384]{1,0:T(8,128)S(1)}, f32[32]{0:T(128)S(1)}) all-reduce(f32[32,384]{1,0:T(8,128)S(1)} %fusion.12, f32[32]{0:T(128)S(1)} %reduce_sum.46), channel_id=1, replica_groups=mesh['tm'=32,'neur'=8] {'neur'}, use_global_device_ids=true, to_apply=%region_0.0 | all-reduce | flops 12320 | bytes 98560 | tf_op jit(solution)/shard_map/psum | solution.py:40
  70.5 0.7 constant_dynamic-update-slice_fusion.31
  71.3 9.2 %collective-permute-start.2 = (bf16[32,15]{1,0:T(8,128)(2,1)S(1)}, bf16[32,15]{1,0:T(8,128)(2,1)S(1)}, u32[]{:S(2)}, u32[]{:S(2)}) collective-permute-start(bf16[32,15]{1,0:T(8,128)(2,1)S(1)} %slice.241), channel_id=1, source_target_pairs={{0,8},{8,16},{16,24},{24,32},{32,40},{40,48},{48,56},{56,64},{64,7... | collective-permute-start | bytes 2888 | tf_op jit(solution)/shard_map/ppermute | solution.py:13
  80.5 0.6 collective-permute-done.2
  81.1 0.1 constant_dynamic-update-slice_fusion.30
  81.4 0.1 constant_dynamic-update-slice_fusion.27
  81.4 0.1 constant_dynamic-update-slice_fusion.26
  81.5 0.1 constant_dynamic-update-slice_fusion.25
  81.6 0.1 constant_dynamic-update-slice_fusion.24
  81.7 0.1 constant_dynamic-update-slice_fusion.23
  81.8 0.1 constant_dynamic-update-slice_fusion.22
  81.9 0.1 constant_dynamic-update-slice_fusion.21
  82.0 0.1 constant_dynamic-update-slice_fusion.20
  82.1 0.1 constant_dynamic-update-slice_fusion.19
  82.2 0.1 constant_dynamic-update-slice_fusion.18
  82.2 0.1 constant_dynamic-update-slice_fusion.17
  82.3 0.1 constant_dynamic-update-slice_fusion.16
  82.4 7.6 %convert_reduce_fusion = (f32[384]{0:T(512)S(1)}, f32[384]{0:T(512)S(1)}, f32[6400,384]{0,1:T(8,128)S(1)}) fusion(bf16[6400,384]{0,1:T(8,128)(2,1)} %copy.25, bf16[512,384]{1,0:T(8,128)(2,1)S(1)} %constant_dynamic-update-slice_fusion.16, bf16[6400,512]{1,0:T(8,128)(2,1)} %param.4), kind=kOutput, calls=%fused_computation | convolution fusion | flops 2533784576 | bytes 21695488 | tf_op jit(solution)/shard_map/dot_general | solution.py:46
  90.1 6.8 %fusion.7 = f32[6400,512]{1,0:T(8,128)} fusion(bf16[512,384]{1,0:T(8,128)(2,1)S(1)} %constant_dynamic-update-slice_fusion.16, f32[6400,384]{0,1:T(8,128)S(1)} %get-tuple-element.12, bf16[6400,384]{0,1:T(8,128)(2,1)S(1)} %bitcast.20), kind=kOutput, calls=%fused_computation.15 | convolution fusion | flops 2523955200 | bytes 28246016 | tf_op jit(solution)/shard_map/dot_general | solution.py:56
  96.9 10.7 %all-reduce = (f32[384]{0:T(512)S(1)}, f32[384]{0:T(512)S(1)}) all-reduce(f32[384]{0:T(512)S(1)} %get-tuple-element.4, f32[384]{0:T(512)S(1)} %get-tuple-element.3), channel_id=1, replica_groups=mesh['tm'=32,'neur'=8] {'neur'}, use_global_device_ids=true, to_apply=%region_8.0 | all-reduce | flops 768 | bytes 6144 | tf_op jit(solution)/shard_map/psum | solution.py:50
  107.6 0.6 div.32
  108.2 0.1 convert_reduce_fusion.2
  108.3 67.6 %psum.37 = f32[512]{0:T(512)S(1)} all-reduce(f32[512]{0:T(512)S(1)} %convert_reduce_fusion.2), channel_id=1, replica_groups=mesh['tm'=32,'neur'=8] {'tm'}, use_global_device_ids=true, to_apply=%region_6.0 | all-reduce | flops 512 | bytes 4096 | tf_op jit(solution)/shard_map/psum | solution.py:54
  175.9 33.5 %reduce-scatter.2.cloned.1.call-done = f32[200,512]{1,0:T(8,128)} async-done(((f32[6400,512]{1,0:T(8,128)}), f32[200,512]{1,0:T(8,128)}) %reduce-scatter.2.cloned.1.call-update) | async-done | bytes 409616 | tf_op jit(solution)/shard_map/reduce_scatter | solution.py:55
  209.4 1.9 multiply_divide_fusion
  (26 shorter events, 0.8 us)
Async XLA Ops:
  7.2 13.7 %copy-start = (bf16[32,384]{1,0:T(8,128)(2,1)S(1)}, bf16[32,384]{1,0:T(8,128)(2,1)}, u32[]{:S(2)}) copy-start(bf16[32,384]{1,0:T(8,128)(2,1)} %param.5) | copy-start | bytes 73732
  7.2 202.2 %reduce-scatter.2.cloned.1.call-start = ((), (), s32[]{:S(2)}) async-start(), calls=%async_computation.1 | async-start | bytes 13516800 | tf_op jit(solution)/shard_map/reduce_scatter | solution.py:55
  8.0 12.8 %collective-permute-start = (bf16[32,15]{1,0:T(8,128)(2,1)S(1)}, bf16[32,15]{1,0:T(8,128)(2,1)S(1)}, u32[]{:S(2)}, u32[]{:S(2)}) collective-permute-start(bf16[32,15]{1,0:T(8,128)(2,1)S(1)} %slice.147), channel_id=1, source_target_pairs={{0,8},{8,16},{16,24},{24,32},{32,40},{40,48},{48,56},{56,64},{64,7... | collective-permute-start | bytes 2888 | tf_op jit(solution)/shard_map/ppermute | solution.py:13
  21.2 11.0 %slice-start = ((s8[6553600]{0:T(1024)(128)(4,1)}), s8[4194304]{0:T(1024)(128)(4,1)S(1)}, s32[]{:S(2)}) async-start(s8[6553600]{0:T(1024)(128)(4,1)} %bitcast.17), calls=%async_computation.2 | async-start | bytes 8388608
  22.2 10.1 %slice-start.1 = ((s8[6553600]{0:T(1024)(128)(4,1)}), s8[2359296]{0:T(1024)(128)(4,1)S(1)}, s32[]{:S(2)}) async-start(s8[6553600]{0:T(1024)(128)(4,1)} %bitcast.17), calls=%async_computation.3 | async-start | bytes 4718592
  30.0 2.2 %copy-start.1 = (bf16[6400,384]{0,1:T(8,128)(2,1)}, bf16[6400,384]{0,1:T(8,128)(2,1)S(1)}, u32[]{:S(2)}) copy-start(bf16[6400,384]{0,1:T(8,128)(2,1)S(1)} %fusion) | copy-start | bytes 14745604
  30.0 7.1 %collective-permute-start.1 = (bf16[6400,15]{0,1:T(8,128)(2,1)S(1)}, bf16[6400,15]{0,1:T(8,128)(2,1)S(1)}, u32[]{:S(2)}, u32[]{:S(2)}) collective-permute-start(bf16[6400,15]{0,1:T(8,128)(2,1)S(1)} %slice.224), channel_id=1, source_target_pairs={{8,0},{16,8},{24,16},{32,24},{40,32},{48,40},{56,48},{64,56},{72,6... | collective-permute-start | bytes 576008 | tf_op jit(solution)/shard_map/ppermute | solution.py:13
  44.2 45.8 %slice-start.2 = ((s8[4915200]{0:T(1024)(128)(4,1)}), s8[720896]{0:T(1024)(128)(4,1)S(1)}, s32[]{:S(2)}) async-start(s8[4915200]{0:T(1024)(128)(4,1)} %bitcast.19), calls=%async_computation.4 | async-start | bytes 1441792
  71.3 9.8 %collective-permute-start.2 = (bf16[32,15]{1,0:T(8,128)(2,1)S(1)}, bf16[32,15]{1,0:T(8,128)(2,1)S(1)}, u32[]{:S(2)}, u32[]{:S(2)}) collective-permute-start(bf16[32,15]{1,0:T(8,128)(2,1)S(1)} %slice.241), channel_id=1, source_target_pairs={{0,8},{8,16},{16,24},{24,32},{32,40},{40,48},{48,56},{56,64},{64,7... | collective-permute-start | bytes 2888 | tf_op jit(solution)/shard_map/ppermute | solution.py:13
  82.4 7.7 %slice-start.3 = ((s8[4915200]{0:T(1024)(128)(4,1)}), s8[4194304]{0:T(1024)(128)(4,1)S(1)}, s32[]{:S(2)}) async-start(s8[4915200]{0:T(1024)(128)(4,1)} %bitcast.19), calls=%async_computation.5 | async-start | bytes 8388608
Sparse Core Ops, SparseCore 0:
  97.0 112.3 reduce-scatter.1
where the time goes:
time: 219 us; the launch traced here: 218 us
  blocking collectives  104 us (47%)
  waiting for transfers between devices  38 us (17%)
  matrix products  29 us (13%)
  starting transfers between devices  15.8 us (7%)
  between operations  14.2 us (6%)
  local copies, waits for them, and re-layouts  9.82 us (4%)
  other arithmetic  7.12 us (3%)
    psum x1, blocking collectives, body(): lagsum = lax.psum(lag_part, 'tm')  67.6 us
    reduce_scatter x1, waiting for transfers between devices, body(): lax.psum_scatter(lax.dot_general(ratio_new, stacked_new, (((1,), (1,)), (...  33.5 us
    psum x1, blocking collectives, body(): numer_all, colsum_all = lax.psum((numer, colsum), 'neur')  26 us
    ppermute x3, starting transfers between devices, passed_along(): lax.ppermute(value, axis, [(source, source + steps) for source in range(l...  15.7 us
    psum x1, blocking collectives, body(): diverge_all, mass_all = lax.psum((diverge, mass), 'neur')  10.7 us
    unnamed x14, local copies, waits for them, and re-layouts  8.53 us
    dot_general x1, matrix products, body(): recon = jnp.dot(patterns, stacked, preferred_element_type=jnp.float32)  7.79 us
    dot_general x1, matrix products, body(): jnp.dot(patterns, stacked_new, preferred_element_type=jnp.float32)  7.64 us
  transfers between devices with their start and end apart: 4, of which 3 were waited for; matrix products, arithmetic and copies ran while one was open for 5% of the time, Pallas kernels for 0%

commit v1 on v0

v1 whole, which is shorter than its diff:
```python
import jax
import jax.numpy as jnp
from jax import lax
from jax.experimental import pallas as pl
from jax.experimental.pallas import tpu as pltpu
from jax.sharding import PartitionSpec as P

RANK = 32
LAGS = 16
NX = 4
NY = 4
NZ = 8
NTM = 32
ROWS = 6400
SPAN = 384
HALO = 128
EXT = HALO + SPAN
WIDTH = RANK * LAGS
CHUNKS = NX * NY
CROWS = ROWS // CHUNKS
OWN = CROWS // 2
PADDED = OWN + 8
TILE = 1280
TILES = ROWS // TILE
F32 = jnp.float32
BF16 = jnp.bfloat16
MESH = pl.DeviceIdType.MESH

ORDER = (
    (2, 2), (2, 1), (1, 2), (2, 3), (3, 2), (2, 0), (0, 2), (1, 1),
    (3, 3), (1, 3), (3, 1), (1, 0), (0, 1), (3, 0), (0, 3), (0, 0),
)
WHERE = {pair: i for i, pair in enumerate(ORDER)}


def coded(axis, start):
    return sum(ORDER[start + i][axis] << (2 * i) for i in range(8))


def relative(i):
    i = jnp.int32(i) if isinstance(i, int) else i
    low = i < 8
    shift = 2 * (i % 8)
    codes = [jnp.where(low, coded(axis, 0), coded(axis, 8)) for axis in (0, 1)]
    return [lax.shift_right_logical(code, shift) & 3 for code in codes]


H1L, H2L, H1R, H2R = 0, 8, 16, 24
C1L, C2L, C1R, C2R = 32, 34, 36, 38
PAIR = 40
ZRS, ZAG, ZMF = 56, 63, 70
LHALO, NHALO, HPAIR = 77, 78, 80
NSEM = 81


def dot(a, b):
    return jnp.dot(a, b, preferred_element_type=F32)


def shifted_rows(ext, lag):
    moved = ext if lag == 0 else pltpu.roll(ext, lag, 1)
    return moved[:, HALO:]


def kernel(
    act_hbm, pat_hbm, load_ref, h_ref, w_ref, mis_ref,
    act, pat, stack, stack_t, ratios, gram, lhalo, blocks, nhalo, ext_load, part, zrecv, hz, hz_pair,
    rat, prat, chunks, h1l, h2l, h1r, h2r, c1l, c2l, c1r, c2r, sums, zsums, lag8,
    isem, ssem, rsem,
):
    tm = lax.axis_index("tm")
    z = lax.axis_index("neur")
    x, y, c = tm // (2 * NY), (tm // 2) % NY, tm % 2

    def at(gx, gy):
        return (gx % NX) * (2 * NY) + (gy % NY) * 2 + c

    after, before = (tm + 1) % NTM, (tm + NTM - 1) % NTM
    partner = tm + 1 - 2 * c
    xp, xm, yp, ym = at(x + 1, y), at(x + 3, y), at(x, y + 1), at(x, y + 3)

    def remote(src, dst, number, to_tm, to_z):
        return pltpu.make_async_remote_copy(
            src_ref=src, dst_ref=dst, send_sem=ssem.at[number], recv_sem=rsem.at[number],
            device_id=(to_tm, to_z), device_id_type=MESH,
        )

    def loads(j):
        rows = pl.ds(pl.multiple_of(j * TILE, TILE), TILE)
        return (
            pltpu.make_async_copy(pat_hbm.at[rows], pat.at[rows], isem.at[j, 0]),
            pltpu.make_async_copy(act_hbm.at[rows], act.at[rows], isem.at[j, 1]),
        )

    for j in range(TILES):
        for copy in loads(j):
            copy.start()

    barrier = pltpu.get_barrier_semaphore()
    peers = [(after, z), (before, z), (partner, z), (xp, z), (xm, z), (yp, z), (ym, z)]
    peers += [(tm, (z + d) % NZ) for d in range(1, NZ)]
    for peer in peers:
        pl.semaphore_signal(barrier, inc=1, device_id=peer, device_id_type=MESH)
    pl.semaphore_wait(barrier, len(peers))

    halo_copy = remote(load_ref.at[:, SPAN - HALO :], lhalo, LHALO, after, z)
    halo_copy.start()
    ratios[:, SPAN:] = jnp.ones((TILE, WIDTH - SPAN), BF16)
    gram[...] = jnp.zeros_like(gram)
    halo_copy.wait()
    rim = jnp.where(tm > 0, lhalo[...].astype(F32), 0.0)
    ext = jnp.concatenate([rim, load_ref[...].astype(F32)], axis=1)
    for p in range(NZ):
        ext_load[p] = ext[4 * p : 4 * p + 4]
    for lag in range(LAGS):
        stack[RANK * lag : RANK * (lag + 1)] = shifted_rows(ext, lag).astype(BF16)

    def first(j, carry):
        for copy in loads(j):
            copy.wait()
        rows = pl.ds(pl.multiple_of(j * TILE, TILE), TILE)
        recon = dot(pat[rows], stack[...])
        ratios[:, :SPAN] = (act[rows].astype(F32) / recon).astype(BF16)
        gram[...] += lax.dot_general(
            pat[rows], ratios[...], (((0,), (0,)), ((), ())), preferred_element_type=F32
        )
        return carry

    lax.fori_loop(0, TILES, first, 0)

    lane = lax.broadcasted_iota(jnp.int32, (RANK, HALO), 1)
    numer = jnp.zeros((RANK, EXT), F32)
    colsum = jnp.zeros((RANK, HALO), F32)
    for lag in range(LAGS):
        rows = gram[RANK * lag : RANK * (lag + 1)]
        wide = jnp.concatenate([jnp.zeros((RANK, HALO), F32), rows[:, :SPAN]], axis=1)
        numer = numer + (wide if lag == 0 else pltpu.roll(wide, EXT - lag, 1))
        colsum = colsum + rows[:, SPAN:]
    blocks[0] = numer[:, :HALO]
    blocks[1] = numer[:, EXT - HALO :]
    to_before = remote(blocks.at[0], nhalo.at[0], NHALO, before, z)
    to_after = remote(blocks.at[1], nhalo.at[1], NHALO + 1, after, z)
    to_before.start()
    to_after.start()
    to_before.wait()
    to_after.wait()
    reach = lane >= HALO - (LAGS - 1)
    from_after = jnp.where(reach & (tm < NTM - 1), nhalo[0], 0.0)
    from_before = jnp.where(reach & (tm > 0), nhalo[1], 0.0)
    head = jnp.where(lane < 64, colsum, numer[:, :HALO] + from_before)
    tail = numer[:, EXT - HALO :] + from_after
    numer = jnp.concatenate([head, numer[:, HALO : EXT - HALO], tail], axis=1)
    for p in range(NZ):
        part[p] = numer[4 * p : 4 * p + 4]

    def over_z(src, dst, base):
        return [remote(src(d), dst(d), base + d - 1, tm, (z + d) % NZ) for d in range(1, NZ)]

    scatter = over_z(lambda d: part.at[(z + d) % NZ], lambda d: zrecv.at[d - 1], ZRS)
    for copy in scatter:
        copy.start()
    for copy in scatter:
        copy.wait()
    total = part[z]
    for d in range(1, NZ):
        total = total + zrecv[d - 1]
    hz[z] = ext_load[z] * total / total[:, 0:1]
    gather = over_z(lambda d: hz.at[z], lambda d: hz.at[z], ZAG)
    for copy in gather:
        copy.start()
    for copy in gather:
        copy.wait()
    to_partner = remote(hz, hz_pair, HPAIR, partner, z)
    to_partner.start()

    def fresh_of(ref):
        return jnp.concatenate([ref[p] for p in range(NZ)], axis=0)

    h_ext = fresh_of(hz)
    h_ref[...] = h_ext[:, HALO:]

    def put_stack(full, direct, first_row):
        full = full.astype(BF16).astype(F32)
        for group in range(LAGS // 4):
            rows = [shifted_rows(full, 4 * group + k) for k in range(4)]
            block = jnp.concatenate(rows, axis=0)
            if direct:
                stack[4 * RANK * group : 4 * RANK * (group + 1)] = block.astype(BF16)
            turned = block.T
            stack_t[first_row : first_row + SPAN, HALO * group : HALO * (group + 1)] = turned.astype(BF16)
            lag_rows = jnp.broadcast_to(jnp.sum(turned, axis=0, keepdims=True), (8, HALO))
            if direct:
                lag8[group] = lag_rows
            else:
                lag8[group] = lag8[group] + lag_rows

    put_stack(h_ext, True, 0)
    sums[...] = jnp.zeros_like(sums)

    def pair_copy(i):
        return remote(rat.at[1 - c, i], prat.at[i], PAIR + i, partner, z)

    def make_ratio(i):
        dx, dy = relative(i)
        start = (((x + dx) % NX) * NY + (y + dy) % NY) * CROWS
        rows = pl.ds(pl.multiple_of(start, 16), CROWS)
        wide = act[rows].astype(F32)
        recon = dot(pat[rows], stack[...])
        ratio = wide / recon
        diverge = wide * jnp.log(ratio) - wide + recon
        sums[0] += jnp.sum(diverge.reshape(CROWS // 8, 8, SPAN), axis=0)
        sums[1] += jnp.sum(wide.reshape(CROWS // 8, 8, SPAN), axis=0)
        rat[0, i] = ratio[:OWN].astype(BF16)
        rat[1, i] = ratio[OWN:].astype(BF16)
        pair_copy(i).start()

    make_ratio(0)
    to_partner.wait()
    put_stack(fresh_of(hz_pair), False, SPAN)


    def half(i, step, other, block, base1, base2, recv1, recv2, plus, minus):
        @pl.when(step == 2)
        def _():
            remote(chunks.at[i, block], recv1.at[other, 0], base1 + 2 * other, plus, z).start()
            remote(chunks.at[i, block + 1], recv1.at[other, 1], base1 + 2 * other + 1, minus, z).start()

        for k, (when, to) in enumerate(((1, plus), (3, minus))):

            @pl.when(step == when)
            def _():
                came = remote(chunks.at[i, block], recv1.at[other, k], base1 + 2 * other + k, to, z)
                came.wait_recv()
                chunks[i, block + k] += recv1[other, k]
                remote(
                    chunks.at[i, pl.ds(block, 2)], recv2.at[other, k], base2 + 2 * other + k, to, z
                ).start()

    def make_chunk(i):
        dx, dy = relative(i)
        pair_copy(i).wait_recv()
        made = dot(rat[c, i], stack_t[:SPAN]) + dot(prat[i], stack_t[SPAN:])
        for b in range(4):
            chunks[i, b, :OWN] = made[:, HALO * b : HALO * (b + 1)]
            chunks[i, b, OWN:] = lag8[b]
        half(i, dx, dy, 0, H1L, H2L, h1l, h2l, xp, xm)
        half(i, dy, dx, 2, H1R, H2R, h1r, h2r, yp, ym)

    def second(i, carry):
        make_ratio(i + 1)
        make_chunk(i)
        return carry

    lax.fori_loop(0, CHUNKS - 1, second, 0)

    diverge = jnp.sum(sums[0], axis=0, keepdims=True)
    mass = jnp.sum(sums[1], axis=0, keepdims=True)
    row = lax.broadcasted_iota(jnp.int32, (8, SPAN), 0)
    zsums[0] = jnp.where(row == 0, diverge, mass)
    spread = over_z(lambda d: zsums.at[0], lambda d: zsums.at[d], ZMF)
    for copy in spread:
        copy.start()

    make_chunk(CHUNKS - 1)

    def last_stage(pos, block, base2, recv2, cb1, cb2, crecv1, crecv2, plus, minus):
        def reduced(other):
            i = WHERE[pos(other)]
            for k in range(2):
                remote(
                    chunks.at[i, pl.ds(block, 2)], recv2.at[other, k], base2 + 2 * other + k, plus, z
                ).wait_recv()
            chunks[i, pl.ds(block, 2)] = chunks[i, pl.ds(block, 2)] + recv2[other, 0] + recv2[other, 1]
            return i

        def begin():
            i = reduced(2)
            remote(chunks.at[i, block], crecv1.at[0], cb1, plus, z).start()
            remote(chunks.at[i, block + 1], crecv1.at[1], cb1 + 1, minus, z).start()

        def middle():
            for k, (other, to) in enumerate(((1, plus), (3, minus))):
                i = reduced(other)
                remote(chunks.at[i, block], crecv1.at[k], cb1 + k, to, z).wait_recv()
                chunks[i, block + k] += crecv1[k]
                remote(chunks.at[i, pl.ds(block, 2)], crecv2.at[k], cb2 + k, to, z).start()

        def end():
            i = reduced(0)
            for k in range(2):
                remote(chunks.at[i, pl.ds(block, 2)], crecv2.at[k], cb2 + k, plus, z).wait_recv()
            chunks[i, pl.ds(block, 2)] = chunks[i, pl.ds(block, 2)] + crecv2[0] + crecv2[1]

        return begin, middle, end

    left = last_stage(lambda o: (0, o), 0, H2L, h2l, C1L, C2L, c1l, c2l, yp, ym)
    right = last_stage(lambda o: (o, 0), 2, H2R, h2r, C1R, C2R, c1r, c2r, xp, xm)
    for a, b in zip(left, right):
        a()
        b()

    mine = pl.ds(pl.multiple_of((x * NY + y) * CROWS, 16), CROWS)
    both = pat[mine].astype(F32)
    own = jnp.where(c == 0, both[:OWN], both[OWN:])
    for b in range(4):
        done = chunks[CHUNKS - 1, b]
        w_ref[:, HALO * b : HALO * (b + 1)] = own[:, HALO * b : HALO * (b + 1)] * done[:OWN] / done[OWN : OWN + 1]

    for copy in spread:
        copy.wait()
    everyone = zsums[0]
    for d in range(1, NZ):
        everyone = everyone + zsums[d]
    mis_ref[...] = everyone[0:1] / everyone[1:2]

    to_partner_done = [pair_copy(i) for i in range(CHUNKS)]
    for copy in to_partner_done:
        copy.wait_send()
    for base1, base2, recv1, recv2 in ((H1L, H2L, h1l, h2l), (H1R, H2R, h1r, h2r)):
        for other in range(4):
            for k in range(2):
                remote(chunks.at[0, 0], recv1.at[other, k], base1 + 2 * other + k, xp, z).wait_send()
                remote(chunks.at[0, pl.ds(0, 2)], recv2.at[other, k], base2 + 2 * other + k, xp, z).wait_send()
    for cb1, cb2, crecv1, crecv2 in ((C1L, C2L, c1l, c2l), (C1R, C2R, c1r, c2r)):
        for k in range(2):
            remote(chunks.at[0, 0], crecv1.at[k], cb1 + k, xp, z).wait_send()
            remote(chunks.at[0, pl.ds(0, 2)], crecv2.at[k], cb2 + k, xp, z).wait_send()


def body(activity, patterns, loadings):
    vmem = pl.BlockSpec(memory_space=pltpu.VMEM)
    anywhere = pl.BlockSpec(memory_space=pl.ANY)
    one = (PADDED, HALO)
    h_next, w_next, misfit = pl.pallas_call(
        kernel,
        out_shape=(
            jax.ShapeDtypeStruct((RANK, SPAN), F32),
            jax.ShapeDtypeStruct((OWN, WIDTH), F32),
            jax.ShapeDtypeStruct((1, SPAN), F32),
        ),
        in_specs=[anywhere, anywhere, vmem],
        out_specs=(vmem, vmem, vmem),
        scratch_shapes=[
            pltpu.VMEM((ROWS, SPAN), BF16),
            pltpu.VMEM((ROWS, WIDTH), BF16),
            pltpu.VMEM((WIDTH, SPAN), BF16),
            pltpu.VMEM((2 * SPAN, WIDTH), BF16),
            pltpu.VMEM((TILE, WIDTH), BF16),
            pltpu.VMEM((WIDTH, WIDTH), F32),
            pltpu.VMEM((RANK, HALO), BF16),
            pltpu.VMEM((2, RANK, HALO), F32),
            pltpu.VMEM((2, RANK, HALO), F32),
            pltpu.VMEM((NZ, 4, EXT), F32),
            pltpu.VMEM((NZ, 4, EXT), F32),
            pltpu.VMEM((NZ - 1, 4, EXT), F32),
            pltpu.VMEM((NZ, 4, EXT), F32),
            pltpu.VMEM((NZ, 4, EXT), F32),
            pltpu.VMEM((2, CHUNKS, OWN, SPAN), BF16),
            pltpu.VMEM((CHUNKS, OWN, SPAN), BF16),
            pltpu.VMEM((CHUNKS, 4) + one, F32),
            pltpu.VMEM((4, 2) + one, F32),
            pltpu.VMEM((4, 2, 2) + one, F32),
            pltpu.VMEM((4, 2) + one, F32),
            pltpu.VMEM((4, 2, 2) + one, F32),
            pltpu.VMEM((2,) + one, F32),
            pltpu.VMEM((2, 2) + one, F32),
            pltpu.VMEM((2,) + one, F32),
            pltpu.VMEM((2, 2) + one, F32),
            pltpu.VMEM((2, 8, SPAN), F32),
            pltpu.VMEM((NZ, 8, SPAN), F32),
            pltpu.VMEM((4, 8, HALO), F32),
            pltpu.SemaphoreType.DMA((TILES, 2)),
            pltpu.SemaphoreType.DMA((NSEM,)),
            pltpu.SemaphoreType.DMA((NSEM,)),
        ],
        compiler_params=pltpu.CompilerParams(
            collective_id=0, has_side_effects=True, vmem_limit_bytes=60 * 1024 * 1024
        ),
    )(activity, patterns, loadings)
    return h_next, w_next, misfit.reshape(SPAN)


def solution(mesh):
    return jax.shard_map(
        body,
        mesh=mesh,
        in_specs=(P("neur", "tm"), P("neur", None), P(None, "tm")),
        out_specs=(P(None, "tm"), P(("neur", "tm"), None), P("tm")),
        check_vma=False,
    )
```

time: 219 us -> 86.3 us (0.39)
  blocking collectives: 104 us -> 0 us
  Pallas kernels: 0 us -> 80.9 us
  waiting for transfers between devices: 38 us -> 0 us
  matrix products: 29 us -> 0 us
  starting transfers between devices: 15.8 us -> 0 us
  between operations: 14.2 us -> 0.64 us
  local copies, waits for them, and re-layouts: 9.82 us -> 3.2 us
  other arithmetic: 7.12 us -> 1.27 us
    psum x3 -> x0, blocking collectives: 104 us -> none  [the longest x1 67.6 us: body(): lagsum = lax.psum(lag_part, 'tm')]
    pallas_call x0 -> x1, Pallas kernels: none -> 80.9 us  [body(): pl.pallas_call(kernel, out_shape=(jax.ShapeDtypeStruct((RANK, SPAN), F32)...]
    reduce_scatter x1 -> x0, waiting for transfers between devices: 33.5 us -> none  [body(): lax.psum_scatter(lax.dot_general(ratio_new, stacked_new, (((1,), (1,)), (...]
    dot_general x4 -> x0, matrix products: 29 us -> none  [the longest x1 7.79 us: body(): recon = jnp.dot(patterns, stacked, preferred_element_type=jnp.float32)]
    ppermute x3 -> x0, starting transfers between devices: 15.7 us -> none  [passed_along(): lax.ppermute(value, axis, [(source, source + steps) for source in range(l...]
    unnamed x14 -> x2, local copies, waits for them, and re-layouts: 8.53 us -> 3.2 us
    ppermute x3 -> x0, waiting for transfers between devices: 4.44 us -> none  [passed_along(): lax.ppermute(value, axis, [(source, source + steps) for source in range(l...]
    unnamed x31 -> x0, other arithmetic: 3.14 us -> none
  transfers between devices with their start and end apart: 4 -> 0, of which waited for: 3 -> 0; matrix products, arithmetic and copies ran while one was open for 5% -> 0% of each run, Pallas kernels for 0% -> 0%
where the time goes in v1:
time: 86.3 us; the launch traced here: 86 us
  Pallas kernels  80.9 us (94%)
  local copies, waits for them, and re-layouts  3.2 us (4%)
  other arithmetic  1.27 us (1%)
    pallas_call x1, Pallas kernels, body(): pl.pallas_call(kernel, out_shape=(jax.ShapeDtypeStruct((RANK, SPAN), F32)...  80.9 us
    unnamed x2, local copies, waits for them, and re-layouts  3.2 us

profile of v1, /device:TPU:1, one launch (start us, length us, event | category | flops | bytes accessed | tf_op | source)
XLA Modules:
  0.0 86.0 jit_solution(13103479692729237388)
XLA Ops:
  0.6 80.9 %shard_map.58 = (f32[32,384]{1,0:T(8,128)}, f32[200,512]{1,0:T(8,128)}, f32[1,384]{1,0:T(1,128)}) custom-call(bf16[6400,384]{1,0:T(8,128)(2,1)} %act_hbm.1, bf16[6400,512]{1,0:T(8,128)(2,1)} %pat_hbm.1, bf16[32,384]{1,0:T(8,128)(2,1)} %load_ref.1), custom_call_target="tpu_custom_call" | custom-call | tf_op jit(solution)/shard_map/pallas_call | solution.py:334
  81.5 1.3 %reduce = f32[384]{0:T(512)} reduce(f32[1,384]{1,0:T(1,128)} %get-tuple-element.8, f32[]{:T(128)} %constant), dimensions={0}, to_apply=%get-tuple-element.8.reduce_sub_computation | reduce | bytes 3076 | tf_op jit(solution)/shard_map/pallas_call | solution.py:334
  82.8 1.4 %copy.8 = f32[32,384]{1,0:T(8,128)} copy(f32[32,384]{1,0:T(8,128)} %get-tuple-element.12) | data formatting | bytes 98304
  84.2 1.8 %copy.9 = f32[200,512]{1,0:T(8,128)} copy(f32[200,512]{1,0:T(8,128)} %get-tuple-element.13) | data formatting | bytes 819200

commit v2 on v1

--- a/solution.py
+++ b/solution.py
@@ -22,6 +22,7 @@
 PADDED = OWN + 8
 TILE = 1280
 TILES = ROWS // TILE
+EARLY = 9
 F32 = jnp.float32
 BF16 = jnp.bfloat16
 MESH = pl.DeviceIdType.MESH
@@ -57,6 +58,19 @@
     return jnp.dot(a, b, preferred_element_type=F32)
 
 
+def narrow(block):
+    lag = block[OWN:]
+    high = lag.astype(BF16).astype(F32)
+    row = lax.broadcasted_iota(jnp.int32, (8, HALO), 0)
+    return jnp.concatenate([block[:OWN], jnp.where(row < 4, high, lag - high)], axis=0).astype(BF16)
+
+
+def widen(block):
+    block = block.astype(F32)
+    lag = block[OWN:]
+    return jnp.concatenate([block[:OWN], lag + pltpu.roll(lag, 4, 0)], axis=0)
+
+
 def shifted_rows(ext, lag):
     moved = ext if lag == 0 else pltpu.roll(ext, lag, 1)
     return moved[:, HALO:]
@@ -65,7 +79,7 @@
 def kernel(
     act_hbm, pat_hbm, load_ref, h_ref, w_ref, mis_ref,
     act, pat, stack, stack_t, ratios, gram, lhalo, blocks, nhalo, ext_load, part, zrecv, hz, hz_pair,
-    rat, prat, chunks, h1l, h2l, h1r, h2r, c1l, c2l, c1r, c2r, sums, zsums, lag8,
+    rat, prat, chunks, halved, h1l, h2l, h1r, h2r, c1l, c2l, c1r, c2r, sums, zsums, lag8,
     isem, ssem, rsem,
 ):
     tm = lax.axis_index("tm")
@@ -222,18 +236,20 @@
     def half(i, step, other, block, base1, base2, recv1, recv2, plus, minus):
         @pl.when(step == 2)
         def _():
-            remote(chunks.at[i, block], recv1.at[other, 0], base1 + 2 * other, plus, z).start()
-            remote(chunks.at[i, block + 1], recv1.at[other, 1], base1 + 2 * other + 1, minus, z).start()
+            for k, to in ((0, plus), (1, minus)):
+                halved[i, block + k] = narrow(chunks[i, block + k])
+                remote(halved.at[i, block + k], recv1.at[other, k], base1 + 2 * other + k, to, z).start()
 
         for k, (when, to) in enumerate(((1, plus), (3, minus))):
 
             @pl.when(step == when)
             def _():
-                came = remote(chunks.at[i, block], recv1.at[other, k], base1 + 2 * other + k, to, z)
+                halved[i, block + 1 - k] = narrow(chunks[i, block + 1 - k])
+                came = remote(halved.at[i, block], recv1.at[other, k], base1 + 2 * other + k, to, z)
                 came.wait_recv()
-                chunks[i, block + k] += recv1[other, k]
+                halved[i, block + k] = narrow(chunks[i, block + k] + widen(recv1[other, k]))
                 remote(
-                    chunks.at[i, pl.ds(block, 2)], recv2.at[other, k], base2 + 2 * other + k, to, z
+                    halved.at[i, pl.ds(block, 2)], recv2.at[other, k], base2 + 2 * other + k, to, z
                 ).start()
 
     def make_chunk(i):
@@ -251,7 +267,43 @@
         make_chunk(i)
         return carry
 
-    lax.fori_loop(0, CHUNKS - 1, second, 0)
+    def last_stage(pos, block, base2, recv2, cb1, cb2, crecv1, crecv2, plus, minus):
+        def reduced(other):
+            i = WHERE[pos(other)]
+            for k in range(2):
+                remote(
+                    halved.at[i, pl.ds(block, 2)], recv2.at[other, k], base2 + 2 * other + k, plus, z
+                ).wait_recv()
+            for b in range(2):
+                chunks[i, block + b] += widen(recv2[other, 0, b]) + widen(recv2[other, 1, b])
+            return i
+
+        def begin():
+            i = reduced(2)
+            remote(chunks.at[i, block], crecv1.at[0], cb1, plus, z).start()
+            remote(chunks.at[i, block + 1], crecv1.at[1], cb1 + 1, minus, z).start()
+
+        def middle():
+            for k, (other, to) in enumerate(((1, plus), (3, minus))):
+                i = reduced(other)
+                remote(chunks.at[i, block], crecv1.at[k], cb1 + k, to, z).wait_recv()
+                chunks[i, block + k] += crecv1[k]
+                remote(chunks.at[i, pl.ds(block, 2)], crecv2.at[k], cb2 + k, to, z).start()
+
+        def end():
+            i = reduced(0)
+            for k in range(2):
+                remote(chunks.at[i, pl.ds(block, 2)], crecv2.at[k], cb2 + k, plus, z).wait_recv()
+            chunks[i, pl.ds(block, 2)] = chunks[i, pl.ds(block, 2)] + crecv2[0] + crecv2[1]
+
+        return begin, middle, end
+
+    left = last_stage(lambda o: (0, o), 0, H2L, h2l, C1L, C2L, c1l, c2l, yp, ym)
+    right = last_stage(lambda o: (o, 0), 2, H2R, h2r, C1R, C2R, c1r, c2r, xp, xm)
+    lax.fori_loop(0, EARLY, second, 0)
+    for begin in (left[0], right[0]):
+        begin()
+    lax.fori_loop(EARLY, CHUNKS - 1, second, 0)
 
     diverge = jnp.sum(sums[0], axis=0, keepdims=True)
     mass = jnp.sum(sums[1], axis=0, keepdims=True)
@@ -261,43 +313,12 @@
     for copy in spread:
         copy.start()
 
+    for middle in (left[1], right[1]):
+        middle()
     make_chunk(CHUNKS - 1)
-
-    def last_stage(pos, block, base2, recv2, cb1, cb2, crecv1, crecv2, plus, minus):
-        def reduced(other):
-            i = WHERE[pos(other)]
-            for k in range(2):
-                remote(
-                    chunks.at[i, pl.ds(block, 2)], recv2.at[other, k], base2 + 2 * other + k, plus, z
-                ).wait_recv()
-            chunks[i, pl.ds(block, 2)] = chunks[i, pl.ds(block, 2)] + recv2[other, 0] + recv2[other, 1]
-            return i
-
-        def begin():
-            i = reduced(2)
-            remote(chunks.at[i, block], crecv1.at[0], cb1, plus, z).start()
-            remote(chunks.at[i, block + 1], crecv1.at[1], cb1 + 1, minus, z).start()
-
-        def middle():
-            for k, (other, to) in enumerate(((1, plus), (3, minus))):
-                i = reduced(other)
-                remote(chunks.at[i, block], crecv1.at[k], cb1 + k, to, z).wait_recv()
-                chunks[i, block + k] += crecv1[k]
-                remote(chunks.at[i, pl.ds(block, 2)], crecv2.at[k], cb2 + k, to, z).start()
-
-        def end():
-            i = reduced(0)
-            for k in range(2):
-                remote(chunks.at[i, pl.ds(block, 2)], crecv2.at[k], cb2 + k, plus, z).wait_recv()
-            chunks[i, pl.ds(block, 2)] = chunks[i, pl.ds(block, 2)] + crecv2[0] + crecv2[1]
-
-        return begin, middle, end
-
-    left = last_stage(lambda o: (0, o), 0, H2L, h2l, C1L, C2L, c1l, c2l, yp, ym)
-    right = last_stage(lambda o: (o, 0), 2, H2R, h2r, C1R, C2R, c1r, c2r, xp, xm)
-    for a, b in zip(left, right):
-        a()
-        b()
+    for end in (left[2], right[2]):
+        end()
+
 
     mine = pl.ds(pl.multiple_of((x * NY + y) * CROWS, 16), CROWS)
     both = pat[mine].astype(F32)
@@ -319,8 +340,8 @@
     for base1, base2, recv1, recv2 in ((H1L, H2L, h1l, h2l), (H1R, H2R, h1r, h2r)):
         for other in range(4):
             for k in range(2):
-                remote(chunks.at[0, 0], recv1.at[other, k], base1 + 2 * other + k, xp, z).wait_send()
-                remote(chunks.at[0, pl.ds(0, 2)], recv2.at[other, k], base2 + 2 * other + k, xp, z).wait_send()
+                remote(halved.at[0, 0], recv1.at[other, k], base1 + 2 * other + k, xp, z).wait_send()
+                remote(halved.at[0, pl.ds(0, 2)], recv2.at[other, k], base2 + 2 * other + k, xp, z).wait_send()
     for cb1, cb2, crecv1, crecv2 in ((C1L, C2L, c1l, c2l), (C1R, C2R, c1r, c2r)):
         for k in range(2):
             remote(chunks.at[0, 0], crecv1.at[k], cb1 + k, xp, z).wait_send()
@@ -358,10 +379,11 @@
             pltpu.VMEM((2, CHUNKS, OWN, SPAN), BF16),
             pltpu.VMEM((CHUNKS, OWN, SPAN), BF16),
             pltpu.VMEM((CHUNKS, 4) + one, F32),
-            pltpu.VMEM((4, 2) + one, F32),
-            pltpu.VMEM((4, 2, 2) + one, F32),
-            pltpu.VMEM((4, 2) + one, F32),
-            pltpu.VMEM((4, 2, 2) + one, F32),
+            pltpu.VMEM((CHUNKS, 4) + one, BF16),
+            pltpu.VMEM((4, 2) + one, BF16),
+            pltpu.VMEM((4, 2, 2) + one, BF16),
+            pltpu.VMEM((4, 2) + one, BF16),
+            pltpu.VMEM((4, 2, 2) + one, BF16),
             pltpu.VMEM((2,) + one, F32),
             pltpu.VMEM((2, 2) + one, F32),
             pltpu.VMEM((2,) + one, F32),

time: 86.3 us -> 72.4 us (0.84)
  Pallas kernels: 80.9 us -> 67 us
    pallas_call x1, Pallas kernels: 80.9 us -> 67 us  [body(): pl.pallas_call(kernel, out_shape=(jax.ShapeDtypeStruct((RANK, SPAN), F32)...]
where the time goes in v2:
time: 72.4 us; the launch traced here: 72.2 us
  Pallas kernels  67 us (93%)
  local copies, waits for them, and re-layouts  3.2 us (4%)
  other arithmetic  1.27 us (2%)
    pallas_call x1, Pallas kernels, body(): pl.pallas_call(kernel, out_shape=(jax.ShapeDtypeStruct((RANK, SPAN), F32)...  67 us
    unnamed x2, local copies, waits for them, and re-layouts  3.2 us

profile of v2, /device:TPU:1, one launch (start us, length us, event | category | flops | bytes accessed | tf_op | source)
XLA Modules:
  0.0 72.2 jit_solution(12744348832969723202)
XLA Ops:
  0.6 67.0 %shard_map.58 = (f32[32,384]{1,0:T(8,128)}, f32[200,512]{1,0:T(8,128)}, f32[1,384]{1,0:T(1,128)}) custom-call(bf16[6400,384]{1,0:T(8,128)(2,1)} %act_hbm.1, bf16[6400,512]{1,0:T(8,128)(2,1)} %pat_hbm.1, bf16[32,384]{1,0:T(8,128)(2,1)} %load_ref.1), custom_call_target="tpu_custom_call" | custom-call | tf_op jit(solution)/shard_map/pallas_call | solution.py:355
  67.7 1.3 %reduce = f32[384]{0:T(512)} reduce(f32[1,384]{1,0:T(1,128)} %get-tuple-element.8, f32[]{:T(128)} %constant), dimensions={0}, to_apply=%get-tuple-element.8.reduce_sub_computation | reduce | bytes 3076 | tf_op jit(solution)/shard_map/pallas_call | solution.py:355
  69.0 1.4 %copy.8 = f32[32,384]{1,0:T(8,128)} copy(f32[32,384]{1,0:T(8,128)} %get-tuple-element.12) | data formatting | bytes 98304
  70.4 1.8 %copy.9 = f32[200,512]{1,0:T(8,128)} copy(f32[200,512]{1,0:T(8,128)} %get-tuple-element.13) | data formatting | bytes 819200

commit v3 on v2

--- a/solution.py
+++ b/solution.py
@@ -23,6 +23,7 @@
 TILE = 1280
 TILES = ROWS // TILE
 EARLY = 9
+LEAD = 3
 F32 = jnp.float32
 BF16 = jnp.bfloat16
 MESH = pl.DeviceIdType.MESH
@@ -51,7 +52,8 @@
 PAIR = 40
 ZRS, ZAG, ZMF = 56, 63, 70
 LHALO, NHALO, HPAIR = 77, 78, 80
-NSEM = 81
+EDGE = 81
+NSEM = 97
 
 
 def dot(a, b):
@@ -112,7 +114,7 @@
 
     barrier = pltpu.get_barrier_semaphore()
     peers = [(after, z), (before, z), (partner, z), (xp, z), (xm, z), (yp, z), (ym, z)]
-    peers += [(tm, (z + d) % NZ) for d in range(1, NZ)]
+    peers += [(to, (z + d) % NZ) for to in (tm, after, before) for d in range(1, NZ)]
     for peer in peers:
         pl.semaphore_signal(barrier, inc=1, device_id=peer, device_id_type=MESH)
     pl.semaphore_wait(barrier, len(peers))
@@ -150,22 +152,20 @@
         wide = jnp.concatenate([jnp.zeros((RANK, HALO), F32), rows[:, :SPAN]], axis=1)
         numer = numer + (wide if lag == 0 else pltpu.roll(wide, EXT - lag, 1))
         colsum = colsum + rows[:, SPAN:]
-    blocks[0] = numer[:, :HALO]
-    blocks[1] = numer[:, EXT - HALO :]
-    to_before = remote(blocks.at[0], nhalo.at[0], NHALO, before, z)
-    to_after = remote(blocks.at[1], nhalo.at[1], NHALO + 1, after, z)
-    to_before.start()
-    to_after.start()
-    to_before.wait()
-    to_after.wait()
-    reach = lane >= HALO - (LAGS - 1)
-    from_after = jnp.where(reach & (tm < NTM - 1), nhalo[0], 0.0)
-    from_before = jnp.where(reach & (tm > 0), nhalo[1], 0.0)
-    head = jnp.where(lane < 64, colsum, numer[:, :HALO] + from_before)
-    tail = numer[:, EXT - HALO :] + from_after
-    numer = jnp.concatenate([head, numer[:, HALO : EXT - HALO], tail], axis=1)
+    head = jnp.where(lane < 64, colsum, numer[:, :HALO])
+    mine = jnp.concatenate([head, numer[:, HALO:]], axis=1)
     for p in range(NZ):
-        part[p] = numer[4 * p : 4 * p + 4]
+        blocks[0, p] = numer[4 * p : 4 * p + 4, :HALO]
+        blocks[1, p] = numer[4 * p : 4 * p + 4, EXT - HALO :]
+        part[p] = mine[4 * p : 4 * p + 4]
+
+    edges = [
+        remote(blocks.at[k, (z + d) % NZ], nhalo.at[k, d], EDGE + NZ * k + d, to, (z + d) % NZ)
+        for k, to in enumerate((before, after))
+        for d in range(NZ)
+    ]
+    for copy in edges:
+        copy.start()
 
     def over_z(src, dst, base):
         return [remote(src(d), dst(d), base + d - 1, tm, (z + d) % NZ) for d in range(1, NZ)]
@@ -178,6 +178,17 @@
     total = part[z]
     for d in range(1, NZ):
         total = total + zrecv[d - 1]
+    for copy in edges:
+        copy.wait()
+    near = [nhalo[k, 0] for k in range(2)]
+    for d in range(1, NZ):
+        near = [near[k] + nhalo[k, d] for k in range(2)]
+    reach = lax.broadcasted_iota(jnp.int32, (4, HALO), 1) >= HALO - (LAGS - 1)
+    from_after = jnp.where(reach & (tm < NTM - 1), near[0], 0.0)
+    from_before = jnp.where(reach & (tm > 0), near[1], 0.0)
+    total = jnp.concatenate(
+        [total[:, :HALO] + from_before, total[:, HALO : EXT - HALO], total[:, EXT - HALO :] + from_after], axis=1
+    )
     hz[z] = ext_load[z] * total / total[:, 0:1]
     gather = over_z(lambda d: hz.at[z], lambda d: hz.at[z], ZAG)
     for copy in gather:
@@ -228,7 +239,11 @@
         rat[1, i] = ratio[OWN:].astype(BF16)
         pair_copy(i).start()
 
-    make_ratio(0)
+    def ahead(i, carry):
+        make_ratio(i)
+        return carry
+
+    lax.fori_loop(0, LEAD, ahead, 0)
     to_partner.wait()
     put_stack(fresh_of(hz_pair), False, SPAN)
 
@@ -263,7 +278,11 @@
         half(i, dy, dx, 2, H1R, H2R, h1r, h2r, yp, ym)
 
     def second(i, carry):
-        make_ratio(i + 1)
+        make_ratio(i + LEAD)
+        make_chunk(i)
+        return carry
+
+    def rest(i, carry):
         make_chunk(i)
         return carry
 
@@ -303,7 +322,7 @@
     lax.fori_loop(0, EARLY, second, 0)
     for begin in (left[0], right[0]):
         begin()
-    lax.fori_loop(EARLY, CHUNKS - 1, second, 0)
+    lax.fori_loop(EARLY, CHUNKS - LEAD, second, 0)
 
     diverge = jnp.sum(sums[0], axis=0, keepdims=True)
     mass = jnp.sum(sums[1], axis=0, keepdims=True)
@@ -313,6 +332,7 @@
     for copy in spread:
         copy.start()
 
+    lax.fori_loop(CHUNKS - LEAD, CHUNKS - 1, rest, 0)
     for middle in (left[1], right[1]):
         middle()
     make_chunk(CHUNKS - 1)
@@ -369,8 +389,8 @@
             pltpu.VMEM((TILE, WIDTH), BF16),
             pltpu.VMEM((WIDTH, WIDTH), F32),
             pltpu.VMEM((RANK, HALO), BF16),
-            pltpu.VMEM((2, RANK, HALO), F32),
-            pltpu.VMEM((2, RANK, HALO), F32),
+            pltpu.VMEM((2, NZ, 4, HALO), F32),
+            pltpu.VMEM((2, NZ, 4, HALO), F32),
             pltpu.VMEM((NZ, 4, EXT), F32),
             pltpu.VMEM((NZ, 4, EXT), F32),
             pltpu.VMEM((NZ - 1, 4, EXT), F32),

time: 72.4 us -> 70.5 us (0.974)
  Pallas kernels: 67 us -> 64.8 us
    pallas_call x1, Pallas kernels: 67 us -> 64.8 us  [body(): pl.pallas_call(kernel, out_shape=(jax.ShapeDtypeStruct((RANK, SPAN), F32)...]
where the time goes in v3:
time: 70.5 us; the launch traced here: 69.9 us
  Pallas kernels  64.8 us (92%)
  local copies, waits for them, and re-layouts  3.2 us (5%)
  other arithmetic  1.27 us (2%)
    pallas_call x1, Pallas kernels, body(): pl.pallas_call(kernel, out_shape=(jax.ShapeDtypeStruct((RANK, SPAN), F32)...  64.8 us
    unnamed x2, local copies, waits for them, and re-layouts  3.2 us

profile of v3, /device:TPU:1, one launch (start us, length us, event | category | flops | bytes accessed | tf_op | source)
XLA Modules:
  0.0 69.9 jit_solution(13031972709341550521)
XLA Ops:
  0.6 64.8 %shard_map.58 = (f32[32,384]{1,0:T(8,128)}, f32[200,512]{1,0:T(8,128)}, f32[1,384]{1,0:T(1,128)}) custom-call(bf16[6400,384]{1,0:T(8,128)(2,1)} %act_hbm.1, bf16[6400,512]{1,0:T(8,128)(2,1)} %pat_hbm.1, bf16[32,384]{1,0:T(8,128)(2,1)} %load_ref.1), custom_call_target="tpu_custom_call" | custom-call | tf_op jit(solution)/shard_map/pallas_call | solution.py:375
  65.4 1.3 %reduce = f32[384]{0:T(512)} reduce(f32[1,384]{1,0:T(1,128)} %get-tuple-element.8, f32[]{:T(128)} %constant), dimensions={0}, to_apply=%get-tuple-element.8.reduce_sub_computation | reduce | bytes 3076 | tf_op jit(solution)/shard_map/pallas_call | solution.py:375
  66.7 1.4 %copy.8 = f32[32,384]{1,0:T(8,128)} copy(f32[32,384]{1,0:T(8,128)} %get-tuple-element.12) | data formatting | bytes 98304
  68.1 1.8 %copy.9 = f32[200,512]{1,0:T(8,128)} copy(f32[200,512]{1,0:T(8,128)} %get-tuple-element.13) | data formatting | bytes 819200
